TPU v7x, 256 devices: a whole 4x4x8 slice. The times are simulated.
256 devices in a mesh: row: 32 (over y, z), col: 8 (over x, core).
Axes of the slice: x: 4, y: 4, z: 8, core: 2. Of those that a mesh axis runs over, the one named last changes fastest.
Arguments:
- panel: float32 [8, 32, 256, 256], P(None, 'row', None, 'col'), may hold values from -0.1875 to 0.1875
- slab: bfloat16 [8, 32, 256, 4, 8, 256], P(None, 'row', None, None, 'col'), may hold values from -6 to 6
- cotangent: bfloat16 [8, 32, 256, 4, 8, 256], P(None, 'row', None, None, 'col'), may hold values from -0.0625 to 0.0625
- inverse: float32 [256, 256], replicated, may hold values from -2 to 8, as said below
Outputs:
- updated: bfloat16 [8, 32, 256, 4, 8, 256], P(None, 'row', None, None, 'col')
- grad_panel: float32 [8, 32, 256, 256], P(None, 'row', None, 'col')
- grad_inverse: float32 [256, 256], P(None, 'col')
Inputs may be any that keep to these rules, and one draw needn't show every extreme that they name: `inverse`: lower triangular; diagonal entries between 4 and 8.
All inputs are finite; a program needn't handle non-finite values.
Results may differ from a plain program's by a relative error of at most 0.015.
Values may be sent and summed in bfloat16 or wider, within the bound.
A program may use at most 128 MiB of HBM per device.

v0:
```python
import jax
import jax.numpy as jnp
from jax import lax
from jax.sharding import PartitionSpec as P


def per_device(panel, slab, cotangent, inverse):
    tiles_local = panel.shape[0]
    tile_size = panel.shape[2]
    strip_width = panel.shape[3]
    slab_tiles = slab.shape[3]
    row_count = tiles_local * tile_size
    slab_width = slab_tiles * tile_size
    row_devices = lax.axis_size("row")
    col_devices = lax.axis_size("col")
    row_index = lax.axis_index("row")
    col_index = lax.axis_index("col")
    highest = lax.Precision.HIGHEST
    contract_rows = (((0,), (0,)), ((), ()))
    panel_rows = panel.reshape(row_count, strip_width)
    gathered = lax.all_gather(panel_rows, "col", axis=1, tiled=True)
    factor = jnp.dot(gathered, inverse.T, precision=highest, preferred_element_type=jnp.float32)
    rounded = factor.astype(jnp.bfloat16)
    factor_tiles = rounded.reshape(tiles_local, tile_size, tile_size)
    tile_list = []
    for column_slot in range(slab_tiles):
        tile_index = column_slot * col_devices + col_index
        is_owner = tile_index % row_devices == row_index
        owned_tile = lax.dynamic_index_in_dim(
            factor_tiles, tile_index // row_devices, 0, keepdims=False
        )
        tile_list.append(jnp.where(is_owner, owned_tile, jnp.zeros_like(owned_tile)))
    stacked = jnp.stack(tile_list).reshape(slab_width, tile_size)
    slab_factor = lax.psum(stacked, "row").astype(jnp.float32).astype(jnp.bfloat16)
    slab_rows = slab.reshape(row_count, slab_width)
    product = jnp.dot(rounded, slab_factor.T, preferred_element_type=jnp.float32)
    updated = (slab_rows.astype(jnp.float32) - product).astype(jnp.bfloat16)
    cot_rows = cotangent.reshape(row_count, slab_width)
    factor_grad = -jnp.dot(cot_rows, slab_factor, preferred_element_type=jnp.float32)
    slab_grad = -lax.dot_general(
        cot_rows, rounded, contract_rows, preferred_element_type=jnp.float32
    )
    slab_grad = lax.psum(slab_grad.astype(jnp.bfloat16), "row").astype(jnp.float32)
    grad_tiles = factor_grad.reshape(tiles_local, tile_size, tile_size)
    for column_slot in range(slab_tiles):
        tile_index = column_slot * col_devices + col_index
        is_owner = tile_index % row_devices == row_index
        local_slot = tile_index // row_devices
        current_tile = lax.dynamic_index_in_dim(grad_tiles, local_slot, 0, keepdims=True)
        added_tile = jnp.where(
            is_owner, slab_grad[column_slot * tile_size : (column_slot + 1) * tile_size], 0.0
        )
        grad_tiles = lax.dynamic_update_index_in_dim(
            grad_tiles, current_tile + added_tile[None], local_slot, 0
        )
    factor_grad = grad_tiles.reshape(row_count, tile_size)
    grad_total = lax.psum(factor_grad, "col")
    inverse_strip = lax.dynamic_slice_in_dim(inverse, col_index * strip_width, strip_width, 1)
    grad_panel = jnp.dot(
        grad_total, inverse_strip, precision=highest, preferred_element_type=jnp.float32
    )
    inverse_term = lax.dot_general(
        grad_total, panel_rows, contract_rows, precision=highest, preferred_element_type=jnp.float32
    )
    grad_inverse = lax.psum(inverse_term, "row")
    return (updated.reshape(slab.shape), grad_panel.reshape(panel.shape), grad_inverse)


def solution(mesh):
    in_specs = (
        P(None, "row", None, "col"),
        P(None, "row", None, None, "col", None),
        P(None, "row", None, None, "col", None),
        P(),
    )
    out_specs = (
        P(None, "row", None, None, "col", None),
        P(None, "row", None, "col"),
        P(None, "col"),
    )
    return jax.shard_map(
        per_device, mesh=mesh, in_specs=in_specs, out_specs=out_specs, check_vma=False
    )
```

profile of v0, /device:TPU:0, one launch (start us, length us, event | category | flops | bytes accessed | tf_op | source)
XLA Modules:
  0.0 430.0 jit_solution(7106329265095890)
XLA Ops:
  7.2 1.7 copy.19
  9.1 5.2 %copy.20 = bf16[256,8,4,256]{3,1,2,0:T(8,128)(2,1)} copy(bf16[256,8,4,256]{3,2,1,0:T(4,128)(2,1)} %bitcast.71) | data formatting | bytes 8388608
  14.3 24.5 %all-gather.2.cloned.1.call-done = f32[2048,256]{0,1:T(8,128)} async-done(((f32[2048,32]{0,1:T(8,128)}), f32[2048,256]{0,1:T(8,128)}) %all-gather.2.cloned.1.call-update) | async-done | bytes 2097168 | tf_op jit(solution)/shard_map/all_gather | solution.py:21
  38.8 5.0 %convolution_convert_fusion = bf16[2048,256]{1,0:T(8,128)(2,1)S(1)} fusion(f32[2048,256]{0,1:T(8,128)} %all-gather.2.cloned.1.call-done, f32[256,256]{1,0:T(8,128)S(1)} %copy-done), kind=kOutput, calls=%fused_computation.2 | convolution fusion | flops 1611137024 | bytes 3407872 | tf_op jit(solution)/shard_map/dot_general | solution.py:22
  43.9 4.3 fusion.1
  48.2 0.9 pad_maximum_fusion
  49.1 0.2 all-reduce.4.cloned.1.call-start
  49.3 150.0 %all-reduce.6.cloned.1.call-done = (bf16[1024,256]{1,0:T(8,128)(2,1)}, bf16[1024,256]{0,1:T(8,128)(2,1)}) async-done(((bf16[1024,256]{1,0:T(8,128)(2,1)}, bf16[1024,256]{0,1:T(8,128)(2,1)}), (bf16[1024,256]{1,0:T(8,128)(2,1)}, bf16[1024,256]{0,1:T(8,128)(2,1)})) %all-reduce.6.cloned.1.call-update) | async-done | bytes 1048592 | tf_op jit(solution)/shard_map/psum | solution.py:34
  199.3 3.7 convolution_negate_fusion
  202.9 0.2 copy.24
  203.1 0.9 copy-done.4
  204.0 0.1 convert_element_type.29
  204.1 0.1 fusion.13
  204.2 0.1 fusion.7
  204.4 1.8 copy.14
  206.2 7.0 %copy.18 = f32[256,8,4,256]{3,1,2,0:T(8,128)} copy(bf16[256,8,4,256]{3,2,1,0:T(4,128)(2,1)} %bitcast.70) | data formatting | bytes 12582912
  213.2 6.8 %subtract_convert_fusion = bf16[2048,1024]{1,0:T(8,128)(2,1)} fusion(f32[2048,1024]{1,0:T(8,128)} %bitcast.66, bf16[2048,256]{1,0:T(8,128)(2,1)S(1)} %convolution_convert_fusion, bf16[1024,256]{1,0:T(8,128)(2,1)S(1)} %copy-done.3), kind=kOutput, calls=%fused_computation | convolution fusion | flops 1077936128 | bytes 14155776 | tf_op jit(solution)/shard_map/dot_general | solution.py:36
  220.1 7.9 %reshape.36 = bf16[8,1,256,4,1,256]{5,3,2,0,4,1:T(4,128)(2,1)} reshape(bf16[2048,1024]{1,0:T(8,128)(2,1)} %subtract_convert_fusion) | data formatting | bytes 8388608 | tf_op jit(solution)/shard_map/reshape | solution.py:66
  227.9 46.6 %all-reduce.4.cloned.1.call-done = f32[2048,256]{1,0:T(8,128)} async-done(((f32[2048,256]{1,0:T(8,128)}), f32[2048,256]{1,0:T(8,128)}) %all-reduce.4.cloned.1.call-update) | async-done | bytes 2097168 | tf_op jit(solution)/shard_map/psum | solution.py:57
  274.5 3.8 fusion.14
  278.3 0.1 copy.21
  278.4 0.8 copy.16
  279.2 1.2 fusion.17
  280.4 143.1 %psum.31 = f32[256,32]{0,1:T(8,128)} all-reduce(f32[256,32]{0,1:T(8,128)S(1)} %fusion.17), channel_id=1, replica_groups=mesh['row'=32,'col'=8] {'row'}, use_global_device_ids=true, to_apply=%region_3.4 | all-reduce | flops 8192 | bytes 65536 | tf_op jit(solution)/shard_map/psum | solution.py:65
  (17 shorter events, 0.3 us)
Async XLA Ops:
  7.2 31.7 %copy-start = (f32[256,256]{1,0:T(8,128)S(1)}, f32[256,256]{1,0:T(8,128)}, u32[]{:S(2)}) copy-start(f32[256,256]{1,0:T(8,128)} %param.7) | copy-start | bytes 786436
  7.2 31.7 %all-gather.2.cloned.1.call-start = ((), (), s32[]{:S(2)}) async-start(), calls=%async_computation | async-start | bytes 2359296 | tf_op jit(solution)/shard_map/all_gather | solution.py:21
  9.0 190.3 %all-reduce.6.cloned.1.call-start = ((), (), s32[]{:S(2)}) async-start(), calls=%async_computation.2 | async-start | bytes 2097152 | tf_op jit(solution)/shard_map/psum | solution.py:34
  49.1 225.4 %all-reduce.4.cloned.1.call-start = ((), (), s32[]{:S(2)}) async-start(), calls=%async_computation.1 | async-start | bytes 4194304 | tf_op jit(solution)/shard_map/psum | solution.py:57
  202.9 1.0 copy-start.4
  206.2 7.0 %copy-start.3 = (bf16[1024,256]{1,0:T(8,128)(2,1)S(1)}, bf16[1024,256]{1,0:T(8,128)(2,1)}, u32[]{:S(2)}) copy-start(bf16[1024,256]{1,0:T(8,128)(2,1)} %get-tuple-element.9) | copy-start | bytes 1572868
  227.9 51.3 %copy-start.2 = (f32[4,8,8,256]{3,1,2,0:T(8,128)S(1)}, f32[4,8,8,256]{3,1,2,0:T(8,128)}, u32[]{:S(2)}) copy-start(f32[4,8,8,256]{3,1,2,0:T(8,128)} %copy.19) | copy-start | bytes 786436
  274.5 4.7 %copy-start.1 = (f32[2048,256]{1,0:T(8,128)S(1)}, f32[2048,256]{1,0:T(8,128)}, u32[]{:S(2)}) copy-start(f32[2048,256]{1,0:T(8,128)} %all-reduce.4.cloned.1.call-done) | copy-start | bytes 6291460
Sparse Core Ops, SparseCore 0:
  9.9 28.9 all-gather.1
  49.2 150.0 all-reduce.5
  206.3 68.1 all-reduce.3
where the time goes:
time: 431 us; the launch traced here: 430 us
  waiting for transfers between devices  221 us (51%)
  blocking collectives  143 us (33%)
  local copies, waits for them, and re-layouts  25.5 us (6%)
  matrix products  24.8 us (6%)
  between operations  13.9 us (3%)
    psum x1, waiting for transfers between devices, per_device(): lax.psum(stacked, 'row').astype(jnp.float32).astype(jnp.bfloat16)  150 us
    psum x1, blocking collectives, per_device(): grad_inverse = lax.psum(inverse_term, 'row')  143 us
    psum x1, waiting for transfers between devices, per_device(): grad_total = lax.psum(factor_grad, 'col')  46.6 us
    all_gather x1, waiting for transfers between devices, per_device(): gathered = lax.all_gather(panel_rows, 'col', axis=1, tiled=True)  24.5 us
    unnamed x15, local copies, waits for them, and re-layouts  15.7 us
  transfers between devices with their start and end apart: 3, of which 3 were waited for; matrix products, arithmetic and copies ran while one was open for 6% of the time, Pallas kernels for 0%

commit v1 on v0

--- a/solution.py
+++ b/solution.py
@@ -62,7 +62,11 @@
     inverse_term = lax.dot_general(
         grad_total, panel_rows, contract_rows, precision=highest, preferred_element_type=jnp.float32
     )
-    grad_inverse = lax.psum(inverse_term, "row")
+    grad_inverse = inverse_term
+    for hop in (1, 2, 4, 8, 16):
+        grad_inverse = grad_inverse + lax.ppermute(
+            grad_inverse, "row", [(dev, dev ^ hop) for dev in range(32)]
+        )
     return (updated.reshape(slab.shape), grad_panel.reshape(panel.shape), grad_inverse)
 
 

time: 431 us -> 330 us (0.77)
  blocking collectives: 143 us -> 0 us
  waiting for transfers between devices: 221 us -> 248 us
  starting transfers between devices: 0.3 us -> 14.6 us
    psum x1 -> x0, blocking collectives: 143 us -> none  [per_device(): grad_inverse = lax.psum(inverse_term, 'row')]
    psum x1, waiting for transfers between devices: 46.6 us -> 68.2 us  [per_device(): grad_total = lax.psum(factor_grad, 'col')]
    ppermute x0 -> x5, starting transfers between devices: none -> 14.5 us  [per_device(): lax.ppermute(grad_inverse, 'row', [(dev, dev ^ hop) for dev in range(32)])]
    ppermute x0 -> x5, waiting for transfers between devices: none -> 4.64 us  [per_device(): lax.ppermute(grad_inverse, 'row', [(dev, dev ^ hop) for dev in range(32)])]
  transfers between devices with their start and end apart: 3 -> 8, of which waited for: 3 -> 5; matrix products, arithmetic and copies ran while one was open for 6% -> 9% of each run, Pallas kernels for 0% -> 0%
where the time goes in v1:
time: 330 us; the launch traced here: 329 us
  waiting for transfers between devices  248 us (75%)
  local copies, waits for them, and re-layouts  25.7 us (8%)
  matrix products  24.5 us (7%)
  starting transfers between devices  14.6 us (4%)
  between operations  13.9 us (4%)
    psum x1, waiting for transfers between devices, per_device(): lax.psum(stacked, 'row').astype(jnp.float32).astype(jnp.bfloat16)  150 us
    psum x1, waiting for transfers between devices, per_device(): grad_total = lax.psum(factor_grad, 'col')  68.2 us
    all_gather x1, waiting for transfers between devices, per_device(): gathered = lax.all_gather(panel_rows, 'col', axis=1, tiled=True)  25.1 us
    unnamed x15, local copies, waits for them, and re-layouts  15.7 us
    ppermute x5, starting transfers between devices, per_device(): lax.ppermute(grad_inverse, 'row', [(dev, dev ^ hop) for dev in range(32)])  14.5 us
    reshape x1, local copies, waits for them, and re-layouts, per_device(): updated.reshape(slab.shape)  7.98 us
    dot_general x1, matrix products, per_device(): jnp.dot(rounded, slab_factor.T, preferred_element_type=jnp.float32)  6.64 us
  transfers between devices with their start and end apart: 8, of which 5 were waited for; matrix products, arithmetic and copies ran while one was open for 9% of the time, Pallas kernels for 0%

profile of v1, /device:TPU:0, one launch (start us, length us, event | category | flops | bytes accessed | tf_op | source)
XLA Modules:
  0.0 328.8 jit_solution(5022288563212661238)
XLA Ops:
  7.2 1.7 copy.19
  9.1 5.2 %copy.20 = bf16[256,8,4,256]{3,1,2,0:T(8,128)(2,1)} copy(bf16[256,8,4,256]{3,2,1,0:T(4,128)(2,1)} %bitcast.71) | data formatting | bytes 8388608
  14.3 25.1 %all-gather.2.cloned.1.call-done = f32[2048,256]{0,1:T(8,128)} async-done(((f32[2048,32]{0,1:T(8,128)}), f32[2048,256]{0,1:T(8,128)}) %all-gather.2.cloned.1.call-update) | async-done | bytes 2097168 | tf_op jit(solution)/shard_map/all_gather | solution.py:21
  39.4 5.0 %convolution_convert_fusion = bf16[2048,256]{1,0:T(8,128)(2,1)S(1)} fusion(f32[2048,256]{0,1:T(8,128)} %all-gather.2.cloned.1.call-done, f32[256,256]{1,0:T(8,128)S(1)} %copy-done), kind=kOutput, calls=%fused_computation.2 | convolution fusion | flops 1611137024 | bytes 3407872 | tf_op jit(solution)/shard_map/dot_general | solution.py:22
  44.4 4.3 %fusion.1 = bf16[1024,256]{0,1:T(8,128)(2,1)} fusion(bf16[2048,256]{1,0:T(8,128)(2,1)S(1)} %convolution_convert_fusion, bf16[2048,1024]{1,0:T(8,128)(2,1)} %bitcast.72), kind=kOutput, calls=%fused_computation.6 | convolution fusion | flops 1074266112 | bytes 5767168 | tf_op jit(solution)/shard_map/dot_general | solution.py:40
  48.8 0.9 pad_maximum_fusion
  49.7 150.2 %all-reduce.6.cloned.1.call-done = (bf16[1024,256]{1,0:T(8,128)(2,1)}, bf16[1024,256]{0,1:T(8,128)(2,1)}) async-done(((bf16[1024,256]{1,0:T(8,128)(2,1)}, bf16[1024,256]{0,1:T(8,128)(2,1)}), (bf16[1024,256]{1,0:T(8,128)(2,1)}, bf16[1024,256]{0,1:T(8,128)(2,1)})) %all-reduce.6.cloned.1.call-update) | async-done | bytes 1048592 | tf_op jit(solution)/shard_map/psum | solution.py:34
  199.9 3.7 %convolution_negate_fusion = f32[256,2048]{1,0:T(8,128)S(1)} fusion(bf16[1024,256]{1,0:T(8,128)(2,1)} %get-tuple-element.9, bf16[2048,1024]{1,0:T(8,128)(2,1)} %bitcast.73), kind=kOutput, calls=%fused_computation.1 | convolution fusion | flops 1074266112 | bytes 6815744 | tf_op jit(solution)/shard_map/dot_general | solution.py:39
  203.8 0.9 copy-done.4
  205.0 1.8 copy.14
  206.8 68.2 %all-reduce.4.cloned.1.call-done = f32[2048,256]{1,0:T(8,128)} async-done(((f32[2048,256]{1,0:T(8,128)}), f32[2048,256]{1,0:T(8,128)}) %all-reduce.4.cloned.1.call-update) | async-done | bytes 2097168 | tf_op jit(solution)/shard_map/psum | solution.py:57
  275.1 2.8 fusion.17
  277.9 1.6 collective-permute-start
  279.5 2.4 collective-permute-done
  281.9 2.5 collective-permute-start.1
  284.4 2.3 collective-permute-done.1
  286.7 5.7 %collective-permute-start.2 = (f32[256,32]{0,1:T(8,128)S(1)}, f32[256,32]{0,1:T(8,128)S(1)}, u32[]{:S(2)}, u32[]{:S(2)}) collective-permute-start(f32[256,32]{0,1:T(8,128)S(1)} %add.109), channel_id=1, source_target_pairs={{0,32},{8,40},{16,48},{24,56},{32,0},{40,8},{48,16},{56,24},{64,96... | collective-permute-start | bytes 98312 | tf_op jit(solution)/shard_map/ppermute | solution.py:67
  292.4 7.0 %copy.18 = f32[256,8,4,256]{3,1,2,0:T(8,128)} copy(bf16[256,8,4,256]{3,2,1,0:T(4,128)(2,1)} %bitcast.70) | data formatting | bytes 12582912
  299.5 1.8 collective-permute-start.3
  301.2 6.6 %subtract_convert_fusion = bf16[2048,1024]{1,0:T(8,128)(2,1)} fusion(f32[2048,1024]{1,0:T(8,128)} %bitcast.66, bf16[2048,256]{1,0:T(8,128)(2,1)S(1)} %convolution_convert_fusion, bf16[1024,256]{1,0:T(8,128)(2,1)S(1)} %copy-done.3), kind=kOutput, calls=%fused_computation | convolution fusion | flops 1077936128 | bytes 14155776 | tf_op jit(solution)/shard_map/dot_general | solution.py:36
  307.9 8.0 %reshape.36 = bf16[8,1,256,4,1,256]{5,3,2,0,4,1:T(4,128)(2,1)} reshape(bf16[2048,1024]{1,0:T(8,128)(2,1)} %subtract_convert_fusion) | data formatting | bytes 8388608 | tf_op jit(solution)/shard_map/reshape | solution.py:70
  315.8 2.8 collective-permute-start.4
  318.6 2.1 fusion.14
  320.8 0.8 copy.16
  (31 shorter events, 1.5 us)
Async XLA Ops:
  7.2 32.2 %copy-start = (f32[256,256]{1,0:T(8,128)S(1)}, f32[256,256]{1,0:T(8,128)}, u32[]{:S(2)}) copy-start(f32[256,256]{1,0:T(8,128)} %param.7) | copy-start | bytes 786436
  7.2 32.2 %all-gather.2.cloned.1.call-start = ((), (), s32[]{:S(2)}) async-start(), calls=%async_computation | async-start | bytes 2359296 | tf_op jit(solution)/shard_map/all_gather | solution.py:21
  9.0 190.9 %all-reduce.6.cloned.1.call-start = ((), (), s32[]{:S(2)}) async-start(), calls=%async_computation.2 | async-start | bytes 2097152 | tf_op jit(solution)/shard_map/psum | solution.py:34
  49.7 225.4 %all-reduce.4.cloned.1.call-start = ((), (), s32[]{:S(2)}) async-start(), calls=%async_computation.1 | async-start | bytes 4194304 | tf_op jit(solution)/shard_map/psum | solution.py:57
  203.6 1.0 copy-start.4
  206.8 68.3 %copy-start.2 = (f32[4,8,8,256]{3,1,2,0:T(8,128)S(1)}, f32[4,8,8,256]{3,1,2,0:T(8,128)}, u32[]{:S(2)}) copy-start(f32[4,8,8,256]{3,1,2,0:T(8,128)} %copy.19) | copy-start | bytes 786436
  277.9 4.0 %collective-permute-start = (f32[256,32]{0,1:T(8,128)S(1)}, f32[256,32]{0,1:T(8,128)S(1)}, u32[]{:S(2)}, u32[]{:S(2)}) collective-permute-start(f32[256,32]{0,1:T(8,128)S(1)} %fusion.17), channel_id=1, source_target_pairs={{0,8},{8,0},{16,24},{24,16},{32,40},{40,32},{48,56},{56,48},{64,72... | collective-permute-start | bytes 98312 | tf_op jit(solution)/shard_map/ppermute | solution.py:67
  281.9 4.8 %collective-permute-start.1 = (f32[256,32]{0,1:T(8,128)S(1)}, f32[256,32]{0,1:T(8,128)S(1)}, u32[]{:S(2)}, u32[]{:S(2)}) collective-permute-start(f32[256,32]{0,1:T(8,128)S(1)} %add.108), channel_id=1, source_target_pairs={{0,16},{8,24},{16,0},{24,8},{32,48},{40,56},{48,32},{56,40},{64,80... | collective-permute-start | bytes 98312 | tf_op jit(solution)/shard_map/ppermute | solution.py:67
  286.7 12.8 %collective-permute-start.2 = (f32[256,32]{0,1:T(8,128)S(1)}, f32[256,32]{0,1:T(8,128)S(1)}, u32[]{:S(2)}, u32[]{:S(2)}) collective-permute-start(f32[256,32]{0,1:T(8,128)S(1)} %add.109), channel_id=1, source_target_pairs={{0,32},{8,40},{16,48},{24,56},{32,0},{40,8},{48,16},{56,24},{64,96... | collective-permute-start | bytes 98312 | tf_op jit(solution)/shard_map/ppermute | solution.py:67
  292.4 8.8 %copy-start.3 = (bf16[1024,256]{1,0:T(8,128)(2,1)S(1)}, bf16[1024,256]{1,0:T(8,128)(2,1)}, u32[]{:S(2)}) copy-start(bf16[1024,256]{1,0:T(8,128)(2,1)} %get-tuple-element.9) | copy-start | bytes 1572868
  299.5 16.4 %collective-permute-start.3 = (f32[256,32]{0,1:T(8,128)S(1)}, f32[256,32]{0,1:T(8,128)S(1)}, u32[]{:S(2)}, u32[]{:S(2)}) collective-permute-start(f32[256,32]{0,1:T(8,128)S(1)} %add.110), channel_id=1, source_target_pairs={{0,64},{8,72},{16,80},{24,88},{32,96},{40,104},{48,112},{56,120},{... | collective-permute-start | bytes 98312 | tf_op jit(solution)/shard_map/ppermute | solution.py:67
  307.9 10.8 %copy-start.1 = (f32[2048,256]{1,0:T(8,128)S(1)}, f32[2048,256]{1,0:T(8,128)}, u32[]{:S(2)}) copy-start(f32[2048,256]{1,0:T(8,128)} %all-reduce.4.cloned.1.call-done) | copy-start | bytes 6291460
  315.8 5.8 %collective-permute-start.4 = (f32[256,32]{0,1:T(8,128)S(1)}, f32[256,32]{0,1:T(8,128)S(1)}, u32[]{:S(2)}, u32[]{:S(2)}) collective-permute-start(f32[256,32]{0,1:T(8,128)S(1)} %add.111), channel_id=1, source_target_pairs={{0,128},{8,136},{16,144},{24,152},{32,160},{40,168},{48,176},{56,1... | collective-permute-start | bytes 98312 | tf_op jit(solution)/shard_map/ppermute | solution.py:67
Sparse Core Ops, SparseCore 0:
  10.4 28.9 all-gather.1
  49.8 150.0 all-reduce.5
  207.0 68.0 all-reduce.3

commit v2 on v0

--- a/solution.py
+++ b/solution.py
@@ -18,7 +18,9 @@
     highest = lax.Precision.HIGHEST
     contract_rows = (((0,), (0,)), ((), ()))
     panel_rows = panel.reshape(row_count, strip_width)
-    gathered = lax.all_gather(panel_rows, "col", axis=1, tiled=True)
+    gathered = jnp.concatenate(
+        lax.all_to_all(jnp.stack([panel_rows] * lax.axis_size("col")), "col", 0, 0), axis=1
+    )
     factor = jnp.dot(gathered, inverse.T, precision=highest, preferred_element_type=jnp.float32)
     rounded = factor.astype(jnp.bfloat16)
     factor_tiles = rounded.reshape(tiles_local, tile_size, tile_size)

time: 431 us -> 431 us (level)
    all_gather x1 -> x0, waiting for transfers between devices: 24.5 us -> none  [per_device(): gathered = lax.all_gather(panel_rows, 'col', axis=1, tiled=True)]
    all_to_all x0 -> x1, waiting for transfers between devices: none -> 21.8 us  [per_device(): lax.all_to_all(jnp.stack([panel_rows] * lax.axis_size('col')), 'col', 0, 0)]
    unnamed x15 -> x17, local copies, waits for them, and re-layouts: 15.7 us -> 15 us
where the time goes in v2:
time: 431 us; the launch traced here: 430 us
  waiting for transfers between devices  218 us (51%)
  blocking collectives  143 us (33%)
  local copies, waits for them, and re-layouts  26.4 us (6%)
  matrix products  23.2 us (5%)
  between operations  14.2 us (3%)
    psum x1, waiting for transfers between devices, per_device(): lax.psum(stacked, 'row').astype(jnp.float32).astype(jnp.bfloat16)  150 us
    psum x1, blocking collectives, per_device(): grad_inverse = lax.psum(inverse_term, 'row')  143 us
    psum x1, waiting for transfers between devices, per_device(): grad_total = lax.psum(factor_grad, 'col')  46.5 us
    all_to_all x1, waiting for transfers between devices, per_device(): lax.all_to_all(jnp.stack([panel_rows] * lax.axis_size('col')), 'col', 0, 0)  21.8 us
    unnamed x17, local copies, waits for them, and re-layouts  15 us
  transfers between devices with their start and end apart: 3, of which 3 were waited for; matrix products, arithmetic and copies ran while one was open for 6% of the time, Pallas kernels for 0%

profile of v2, /device:TPU:0, one launch (start us, length us, event | category | flops | bytes accessed | tf_op | source)
XLA Modules:
  0.0 430.2 jit_solution(2429456965574969300)
XLA Ops:
  7.2 1.0 copy.19
  8.2 1.6 stack.4
  9.8 3.6 all-to-all-start
  13.5 5.2 %copy.20 = bf16[256,8,4,256]{3,1,2,0:T(8,128)(2,1)} copy(bf16[256,8,4,256]{3,2,1,0:T(4,128)(2,1)} %bitcast.75) | data formatting | bytes 8388608
  18.8 21.8 %all-to-all-done = f32[8,2048,32]{1,2,0:T(8,128)S(1)} async-done(((f32[8,2048,32]{1,2,0:T(8,128)}), f32[8,2048,32]{1,2,0:T(8,128)S(1)}, u32[]{:S(2)}, u32[]{:S(2)}) %all-to-all-start) | async-done | bytes 2097184 | tf_op jit(solution)/shard_map/all_to_all | solution.py:22
  40.5 3.4 convolution_convert_fusion
  44.0 4.3 fusion.1
  48.3 0.9 pad_maximum_fusion
  49.2 0.2 all-reduce.4.cloned.1.call-start
  49.4 149.8 %all-reduce.6.cloned.1.call-done = (bf16[1024,256]{1,0:T(8,128)(2,1)}, bf16[1024,256]{0,1:T(8,128)(2,1)}) async-done(((bf16[1024,256]{1,0:T(8,128)(2,1)}, bf16[1024,256]{0,1:T(8,128)(2,1)}), (bf16[1024,256]{1,0:T(8,128)(2,1)}, bf16[1024,256]{0,1:T(8,128)(2,1)})) %all-reduce.6.cloned.1.call-update) | async-done | bytes 1048592 | tf_op jit(solution)/shard_map/psum | solution.py:36
  199.2 3.7 convolution_negate_fusion
  202.9 0.2 copy.24
  203.1 0.9 copy-done.5
  203.9 0.1 convert_element_type.29
  204.3 1.8 copy.14
  206.2 7.0 %copy.18 = f32[256,8,4,256]{3,1,2,0:T(8,128)} copy(bf16[256,8,4,256]{3,2,1,0:T(4,128)(2,1)} %bitcast.74) | data formatting | bytes 12582912
  213.2 6.8 %subtract_convert_fusion = bf16[2048,1024]{1,0:T(8,128)(2,1)} fusion(f32[2048,1024]{1,0:T(8,128)} %bitcast.69, bf16[2048,256]{1,0:T(8,128)(2,1)S(1)} %convolution_convert_fusion, bf16[1024,256]{1,0:T(8,128)(2,1)S(1)} %copy-done.4), kind=kOutput, calls=%fused_computation | convolution fusion | flops 1077936128 | bytes 14155776 | tf_op jit(solution)/shard_map/dot_general | solution.py:38
  220.0 7.9 %reshape.43 = bf16[8,1,256,4,1,256]{5,3,2,0,4,1:T(4,128)(2,1)} reshape(bf16[2048,1024]{1,0:T(8,128)(2,1)} %subtract_convert_fusion) | data formatting | bytes 8388608 | tf_op jit(solution)/shard_map/reshape | solution.py:68
  227.9 46.5 %all-reduce.4.cloned.1.call-done = f32[2048,256]{1,0:T(8,128)} async-done(((f32[2048,256]{1,0:T(8,128)}), f32[2048,256]{1,0:T(8,128)}) %all-reduce.4.cloned.1.call-update) | async-done | bytes 2097168 | tf_op jit(solution)/shard_map/psum | solution.py:59
  274.4 3.8 fusion.14
  278.2 0.1 copy.21
  278.3 0.8 copy.16
  279.1 1.2 fusion.17
  280.2 143.1 %psum.31 = f32[256,32]{0,1:T(8,128)} all-reduce(f32[256,32]{0,1:T(8,128)S(1)} %fusion.17), channel_id=1, replica_groups=mesh['row'=32,'col'=8] {'row'}, use_global_device_ids=true, to_apply=%region_3.4 | all-reduce | flops 8192 | bytes 65536 | tf_op jit(solution)/shard_map/psum | solution.py:67
  (19 shorter events, 0.4 us)
Async XLA Ops:
  7.2 33.4 %copy-start = (f32[256,256]{1,0:T(8,128)S(1)}, f32[256,256]{1,0:T(8,128)}, u32[]{:S(2)}) copy-start(f32[256,256]{1,0:T(8,128)} %param.7) | copy-start | bytes 786436
  8.2 1.6 copy-start.2
  9.8 30.7 %all-to-all-start = ((f32[8,2048,32]{1,2,0:T(8,128)}), f32[8,2048,32]{1,2,0:T(8,128)S(1)}, u32[]{:S(2)}, u32[]{:S(2)}) async-start(f32[8,2048,32]{1,2,0:T(8,128)} %stack.4), calls=%async_computation | async-start | bytes 4194304 | tf_op jit(solution)/shard_map/all_to_all | solution.py:22
  13.4 185.8 %all-reduce.6.cloned.1.call-start = ((), (), s32[]{:S(2)}) async-start(), calls=%async_computation.2 | async-start | bytes 2097152 | tf_op jit(solution)/shard_map/psum | solution.py:36
  49.2 225.2 %all-reduce.4.cloned.1.call-start = ((), (), s32[]{:S(2)}) async-start(), calls=%async_computation.1 | async-start | bytes 4194304 | tf_op jit(solution)/shard_map/psum | solution.py:59
  202.9 1.0 copy-start.5
  206.1 7.0 %copy-start.4 = (bf16[1024,256]{1,0:T(8,128)(2,1)S(1)}, bf16[1024,256]{1,0:T(8,128)(2,1)}, u32[]{:S(2)}) copy-start(bf16[1024,256]{1,0:T(8,128)(2,1)} %get-tuple-element.9) | copy-start | bytes 1572868
  227.9 51.2 %copy-start.3 = (f32[4,8,8,256]{3,1,2,0:T(8,128)S(1)}, f32[4,8,8,256]{3,1,2,0:T(8,128)}, u32[]{:S(2)}) copy-start(f32[4,8,8,256]{3,1,2,0:T(8,128)} %copy-done.2) | copy-start | bytes 786436
  274.4 4.7 %copy-start.1 = (f32[2048,256]{1,0:T(8,128)S(1)}, f32[2048,256]{1,0:T(8,128)}, u32[]{:S(2)}) copy-start(f32[2048,256]{1,0:T(8,128)} %all-reduce.4.cloned.1.call-done) | copy-start | bytes 6291460
Sparse Core Ops, SparseCore 0:
  49.3 149.8 all-reduce.5
  206.3 68.0 all-reduce.3
